TPU v7x, 32 devices: a whole 2x2x4 slice. The times are simulated.
32 devices in a mesh: gz: 8 (over y, x, core), xy: 4 (over z).
Axes of the slice: x: 2, y: 2, z: 4, core: 2. Of those that a mesh axis runs over, the one named last changes fastest.
Arguments:
- populations: float32 [19, 128, 2048], P(None, 'xy', 'gz'), may hold values from 0.01 to 0.5, as said below
- positions: float32 [3, 262144], P(None, ('gz', 'xy')), may hold values from 0 to 32, as said below
- velocities: float32 [3, 262144], P(None, ('gz', 'xy')), may hold values from -4 to 4
- cells: int32 [262144], P(('gz', 'xy')), may hold values from 0 to 8191, as said below
- partners: int32 [2, 262144], P(None, ('gz', 'xy')), may hold values from -1 to 24575
- counts: int32 [32], P(('gz', 'xy')), may hold values from 1 to 8192, as said below
Outputs:
- new_populations: float32 [19, 128, 2048], P(None, 'xy', 'gz')
- displacement: float32 [3, 262144], P(None, ('gz', 'xy'))
- new_velocities: float32 [3, 262144], P(None, ('gz', 'xy'))
Inputs may be any that keep to these rules, and one draw needn't show every extreme that they name: `populations`: each population lies between half and one and a half times its lattice weight. A live bead's position lies inside its cell: cell (z, w, p) holds the positions with z <= first component < z + 1, and likewise for w and p. `cells`: the cell of the bead within its brick, numbered w * 16 * 16 + z * 16 + p from the brick's corner. `counts`: slots 0 to count - 1 of a brick hold its beads; in every draw some brick is full.
All inputs are finite; a program needn't handle non-finite values.
Results may differ from a plain program's by a relative error of at most 0.00014.
Values sent between devices are 32-bit elements; how exact they have to be, the bound alone decides.
A program may use at most 64 MiB of HBM per device.

v0:
```python
import functools

import jax
import jax.numpy as jnp
from jax import lax
from jax.experimental import pallas as pl
from jax.experimental.pallas import tpu as pltpu
from jax.sharding import PartitionSpec as P

PL = 16
CZ = 16
SUBSTEPS = 3
LANES = 128
GHOST_ROWS = 2

VELOCITIES = (
    (0, 0, 0),
    (1, 0, 0),
    (-1, 0, 0),
    (0, 1, 0),
    (0, -1, 0),
    (0, 0, 1),
    (0, 0, -1),
    (1, 1, 0),
    (-1, -1, 0),
    (1, -1, 0),
    (-1, 1, 0),
    (1, 0, 1),
    (-1, 0, -1),
    (1, 0, -1),
    (-1, 0, 1),
    (0, 1, 1),
    (0, -1, -1),
    (0, 1, -1),
    (0, -1, 1),
)
WEIGHTS = (1.0 / 3.0,) + (1.0 / 18.0,) * 6 + (1.0 / 36.0,) * 12
OPPOSITE = (0, 2, 1, 4, 3, 6, 5, 8, 7, 10, 9, 12, 11, 14, 13, 16, 15, 18, 17)
RELAX_TIME = 0.8
SPRING = 1.0
FRICTION = 0.25
START_SCALE = 2.0**16
MOVE_SCALE = 2.0**15
MOVE_BASE = 32.0
FLOW_SCALE = 2.0**19
FLOW_BASE = 2.0

MESH = pl.DeviceIdType.MESH
F32 = jnp.float32
BF16 = jnp.bfloat16


def moving(component, sign):
    return [m for m in range(19) if VELOCITIES[m][component] == sign]


def project(vector, fields):
    total = None
    for component in range(3):
        if vector[component] != 0:
            term = fields[component] if vector[component] > 0 else -fields[component]
            total = term if total is None else total + term
    return total


def lookup(row, index):
    return jnp.take_along_axis(row, index, axis=1, mode="promise_in_bounds")


def spread(row):
    return jnp.broadcast_to(row, (8, LANES))


def pack(values, scale, base):
    top = float(2**21 - 1)
    fixed = [
        jnp.clip((v + base) * scale, 0.0, top).astype(jnp.int32) if base == 0.0
        else jnp.clip((v + base) * scale + 0.5, 0.0, top).astype(jnp.int32)
        for v in values
    ]
    return (fixed[0] << 11) | (fixed[2] >> 10), (fixed[1] << 11) | (fixed[2] & 1023)


def unpack(first, second):
    return (
        lax.shift_right_logical(first, 11),
        lax.shift_right_logical(second, 11),
        ((first & 2047) << 10) | (second & 1023),
    )


def kernel(
    nz,
    nx,
    pop_ref,
    pos_ref,
    vel_ref,
    cell_ref,
    part_ref,
    count_ref,
    passed,
    dragsum,
    tab,
    vel,
    hi_ref,
    lo_ref,
    ghi_ref,
    glo_ref,
    spr,
    listhi_ref,
    listlo_ref,
    beadflow,
    combined,
    ranksend,
    rankrecv,
    zsend,
    zrecv,
    wsend,
    wrecv,
    gsend,
    grecv,
    ghi_full,
    words_ref,
    inner,
    bonds_ref,
    offset_ref,
    first,
    facing,
    own_rank,
    flow_words,
    send_sems,
    recv_sems,
):
    cross, span = pop_ref.shape[1], pop_ref.shape[2]
    capacity = pos_ref.shape[1]
    rows = capacity // LANES
    me_z, me_x = lax.axis_index("gz"), lax.axis_index("xy")
    up = {"gz": lax.rem(me_z + 1, nz)}
    down = {"gz": lax.rem(me_z + nz - 1, nz)}
    right = {"xy": lax.rem(me_x + 1, nx)}
    left = {"xy": lax.rem(me_x + nx - 1, nx)}

    barrier = pltpu.get_barrier_semaphore()
    for neighbour in (up, down, right, left):
        pl.semaphore_signal(barrier, inc=1, device_id=neighbour, device_id_type=MESH)

    def copy(slot, source, target, device):
        return pltpu.make_async_remote_copy(
            src_ref=source,
            dst_ref=target,
            send_sem=send_sems.at[slot],
            recv_sem=recv_sems.at[slot],
            device_id=device,
            device_id_type=MESH,
        )

    lane = lax.broadcasted_iota(jnp.int32, (cross, LANES), 1)
    for side, sign in enumerate((1, -1)):
        packed = None
        for k, member in enumerate(moving(0, sign)):
            if sign > 0:
                part = pltpu.roll(pop_ref[member, :, span - LANES :], (PL * (k + 1)) % LANES, 1)
            else:
                part = pop_ref[member, :, :LANES]
                part = pltpu.roll(part, PL * k, 1) if k else part
            packed = part if packed is None else jnp.where(lane >= PL * k, part, packed)
        zsend[side] = packed

    for column in range(2):
        for r in range(rows):
            hi_ref[column, r : r + 1, :] = part_ref[column : column + 1, r * LANES : (r + 1) * LANES]
    codes = [hi_ref[column] for column in range(2)]
    names_up = (codes[0] >= 2 * capacity) | (codes[1] >= 2 * capacity)
    names_down = ((codes[0] >= 0) & (codes[0] < capacity)) | ((codes[1] >= 0) & (codes[1] < capacity))
    tri = (
        lax.broadcasted_iota(jnp.int32, (LANES, LANES), 0)
        <= lax.broadcasted_iota(jnp.int32, (LANES, LANES), 1)
    ).astype(F32).astype(BF16)
    below_row = (
        lax.broadcasted_iota(jnp.int32, (rows, rows), 1)
        < lax.broadcasted_iota(jnp.int32, (rows, rows), 0)
    ).astype(F32).astype(BF16)
    wide = GHOST_ROWS * LANES
    wanted = lax.broadcasted_iota(jnp.int32, (rows, wide), 1).astype(F32)
    row_of = lax.broadcasted_iota(jnp.int32, (rows, wide), 0).astype(F32)
    wanted_lane = lax.broadcasted_iota(jnp.int32, (LANES, wide), 1).astype(F32)
    listhi_ref[...] = jnp.full((8, LANES), -1, jnp.int32)
    listlo_ref[...] = jnp.zeros((8, LANES), jnp.int32)
    for side, mask in enumerate((names_up, names_down)):
        flag = mask.astype(F32)
        flag16 = flag.astype(BF16)
        inside = jnp.dot(flag16, tri, preferred_element_type=F32)
        before = jnp.sum(jnp.dot(below_row, flag16, preferred_element_type=F32), axis=1, keepdims=True)
        rank = inside + before
        ranksend[side] = jnp.where(mask, rank - 1.0, 0.0)
        own_rank[side] = jnp.where(mask, rank - 1.0, -1.0).astype(jnp.int32)
        row_end = before + jnp.sum(flag, axis=1, keepdims=True)
        hi = jnp.sum((row_end <= wanted).astype(F32), axis=0, keepdims=True)
        pick = (row_of == hi).astype(F32).astype(BF16)
        table = lax.dot_general(
            rank.astype(BF16), pick, (((0,), (0,)), ((), ())), preferred_element_type=F32
        )
        lo = jnp.sum((table <= wanted_lane).astype(F32), axis=0, keepdims=True)
        hi = hi.astype(jnp.int32)
        lo = jnp.minimum(lo.astype(jnp.int32), LANES - 1)
        for k in range(GHOST_ROWS):
            at = side * GHOST_ROWS + k
            listhi_ref[at : at + 1, :] = hi[:, k * LANES : (k + 1) * LANES]
            listlo_ref[at : at + 1, :] = lo[:, k * LANES : (k + 1) * LANES]

    pl.semaphore_wait(barrier, 4)
    copies = {}
    copies["z0"] = copy(0, zsend.at[0], zrecv.at[0], up)
    copies["z1"] = copy(1, zsend.at[1], zrecv.at[1], down)
    copies["r0"] = copy(2, ranksend.at[0], rankrecv.at[0], up)
    copies["r1"] = copy(3, ranksend.at[1], rankrecv.at[1], down)
    copies["w0"] = copy(4, wsend.at[0], wrecv.at[0], right)
    copies["w1"] = copy(5, wsend.at[1], wrecv.at[1], left)
    for turn in range(SUBSTEPS):
        copies["g0", turn] = copy(6 + 2 * turn, gsend.at[turn], grecv.at[turn, 0], up)
        copies["g1", turn] = copy(7 + 2 * turn, gsend.at[turn], grecv.at[turn, 1], down)
    for name in ("z0", "z1", "r0", "r1"):
        copies[name].start()

    for column in range(2):
        code = codes[column]
        slot = code & (capacity - 1)
        own = (code >= capacity) & (code < 2 * capacity)
        hi_ref[column] = jnp.where(own, slot >> 7, -1)
        lo_ref[column] = slot & (LANES - 1)
        ghi_full[column] = jnp.where(own | (code < 0), 0, code + 1)
    named = [(code >= 0).astype(F32) for code in codes]
    bonds_ref[...] = named[0] + named[1]
    inner[...] = sum(((code >= capacity) & (code < 2 * capacity)).astype(F32) for code in codes)
    offset_ref[...] = sum(
        jnp.where(code >= 2 * capacity, float(CZ), jnp.where((code >= 0) & (code < capacity), -float(CZ), 0.0))
        for code in codes
    )
    for component in range(3):
        for r in range(rows):
            at = slice(r * LANES, (r + 1) * LANES)
            tab[component, r : r + 1, :] = pos_ref[component : component + 1, at]
            vel[component, r : r + 1, :] = vel_ref[component : component + 1, at]

    def sweep(source, hi, lo, width, lines=None, dtype=jnp.int32):
        accs = [jnp.zeros((8, LANES), dtype) for _ in range(width)]
        for r in range(lines or rows):
            hit = hi == r
            for component in range(width):
                accs[component] = jnp.where(hit, lookup(spread(source(component, r)), lo), accs[component])
        return accs

    def packed_row(component, r):
        return words_ref[component, r : r + 1, :]

    def moved_row(component, r):
        return tab[component, r : r + 1, :]

    def send_ghosts(turn):
        listed = sweep(moved_row, listhi_ref[...], listlo_ref[...], 3, dtype=F32)
        for component in range(3):
            gsend[turn, component] = listed[component]
        copies["g0", turn].start()
        copies["g1", turn].start()

    def own_springs(turn):
        scale, base = (START_SCALE, 0.0) if turn == 0 else (MOVE_SCALE, MOVE_BASE)
        words = pack([tab[component] for component in range(3)], scale, base)
        words_ref[0] = words[0]
        words_ref[1] = words[1]

        @pl.loop(0, rows // 8)
        def _(g):
            at = pl.multiple_of(g * 8, 8)
            totals = None
            for column in range(2):
                found = unpack(
                    *sweep(packed_row, hi_ref[column, pl.ds(at, 8), :], lo_ref[column, pl.ds(at, 8), :], 2)
                )
                totals = found if totals is None else [x + y for x, y in zip(totals, found)]
            count = inner[pl.ds(at, 8), :]
            for component in range(3):
                value = totals[component].astype(F32)
                value = (value + 0.5 * count) * (1.0 / scale) if turn == 0 else value * (1.0 / scale) - base * count
                spr[component, pl.ds(at, 8), :] = value

    def ghost_springs(turn):
        near = []
        for component in range(3):
            total = jnp.zeros((8, LANES), F32)
            for column in range(2):
                hi = ghi_ref[column]
                lo = glo_ref[column]
                got = jnp.zeros((8, LANES), F32)
                for r in range(2 * GHOST_ROWS):
                    line = spread(grecv[turn, r // GHOST_ROWS, component, r : r + 1, :])
                    got = jnp.where(hi == r, lookup(line, lo), got)
                total = total + got
            near.append(total)
        for component in range(3):
            facing[component] = near[component]

        @pl.loop(0, rows // 8)
        def _(g):
            at = pl.multiple_of(g * 8, 8)
            totals = [spr[component, pl.ds(at, 8), :] for component in range(3)]
            for side in range(2):
                place = own_rank[side, pl.ds(at, 8), :]
                hi, lo = place >> 7, place & (LANES - 1)
                for k in range(GHOST_ROWS):
                    hit = hi == k
                    r = side * GHOST_ROWS + k
                    for component in range(3):
                        line = spread(facing[component, r : r + 1, :])
                        totals[component] = totals[component] + jnp.where(hit, lookup(line, lo), 0.0)
            for component in range(3):
                spr[component, pl.ds(at, 8), :] = totals[component]

    listed = sweep(
        lambda column, r: ghi_full[column, r : r + 1, :], listhi_ref[...], listlo_ref[...], 2
    )
    for column in range(2):
        ghi_ref[column] = listed[column]

    send_ghosts(0)
    own_springs(0)

    copies["z0"].wait()
    copies["z1"].wait()
    long_lane = lax.broadcasted_iota(jnp.int32, (cross, span), 1)
    plane = long_lane & (PL - 1)
    cross_row = lax.broadcasted_iota(jnp.int32, (cross, span), 0)

    def along(member):
        value = pop_ref[member]
        sign = VELOCITIES[member][0]
        if sign == 0:
            return value
        k = moving(0, sign).index(member)
        if sign > 0:
            got = zrecv[0]
            got = pltpu.roll(got, LANES - PL * k, 1) if k else got
            edge = long_lane < PL
        else:
            got = pltpu.roll(zrecv[1], LANES - PL * (k + 1), 1)
            edge = long_lane >= span - PL
        value = pltpu.roll(value, PL if sign > 0 else span - PL, 1)
        return jnp.where(edge, jnp.concatenate([got] * (span // LANES), axis=1), value)

    across = {}
    for side, sign in enumerate((1, -1)):
        for k, member in enumerate(moving(1, sign)):
            value = along(member)
            passed[member] = value
            across[member] = k
            wsend[side, k : k + 1, :] = value[cross - 1 :, :] if sign > 0 else value[:1, :]
    copies["w0"].start()
    copies["w1"].start()

    copies["r0"].wait()
    copies["r1"].wait()
    combined[...] = rankrecv[0] + rankrecv[1] * 1024.0
    list_row = lax.broadcasted_iota(jnp.int32, (8, LANES), 0)
    for column in range(2):
        code = ghi_ref[column] - 1
        slot = code & (capacity - 1)
        got = sweep(
            lambda component, r: combined[r : r + 1, :],
            jnp.where(code >= 0, slot >> 7, -1),
            slot & (LANES - 1),
            1,
            dtype=F32,
        )[0].astype(jnp.int32)
        above = code >= 2 * capacity
        mine = (code >= 0) & (above == (list_row < GHOST_ROWS)) & (list_row < 2 * GHOST_ROWS)
        rank = jnp.where(above, got >> 10, got & 1023)
        ghi_ref[column] = jnp.where(mine, (rank >> 7) + jnp.where(above, GHOST_ROWS, 0), -1)
        glo_ref[column] = rank & (LANES - 1)

    copies["w0"].wait()
    copies["w1"].wait()
    density = None
    momentum = [None] * 3
    for member in range(19):
        shift_long, shift_cross, shift_plane = VELOCITIES[member]
        if shift_cross != 0:
            value = passed[member]
            side = 0 if shift_cross > 0 else 1
            value = pltpu.roll(value, 1 if shift_cross > 0 else cross - 1, 0)
            edge = cross_row == (0 if shift_cross > 0 else cross - 1)
            k = across[member]
            value = jnp.where(edge, wrecv[side, k : k + 1, :], value)
        else:
            value = along(member)
        if shift_plane != 0:
            value = pltpu.roll(value, 1 if shift_plane > 0 else span - 1, 1)
            border = plane == (0 if shift_plane > 0 else PL - 1)
            value = jnp.where(border, pop_ref[OPPOSITE[member]], value)
        passed[member] = value
        density = value if density is None else density + value
        for component in range(3):
            if VELOCITIES[member][component] != 0:
                term = value if VELOCITIES[member][component] > 0 else -value
                momentum[component] = term if momentum[component] is None else momentum[component] + term
    inverse = 1.0 / density
    words = pack([momentum[component] * inverse for component in range(3)], FLOW_SCALE, FLOW_BASE)
    for half in range(span // LANES):
        for word in range(2):
            flow_words[word, half] = words[word][:, half * LANES : (half + 1) * LANES]

    halves = span // LANES

    def flow_row(component, r):
        line, half = divmod(r, halves)
        return flow_words[component, half, line : line + 1, :]

    @pl.loop(0, rows // 8)
    def _(g):
        at = pl.multiple_of(g * 8, 8)
        cell = cell_ref[pl.ds(at, 8), :]
        found = unpack(*sweep(flow_row, cell >> 7, cell & (LANES - 1), 2, cross * halves))
        for component in range(3):
            beadflow[component, pl.ds(at, 8), :] = (
                found[component].astype(F32) * (1.0 / FLOW_SCALE) - FLOW_BASE
            )

    slot_index = (
        lax.broadcasted_iota(jnp.int32, (rows, LANES), 0) * LANES
        + lax.broadcasted_iota(jnp.int32, (rows, LANES), 1)
    )
    alive = (slot_index < count_ref[0]).astype(F32)
    substep = 1.0 / SUBSTEPS
    for turn in range(SUBSTEPS):
        if turn > 0:
            own_springs(turn)
        copies["g0", turn].wait()
        copies["g1", turn].wait()
        ghost_springs(turn)
        for component in range(3):
            moved = tab[component]
            speed = vel[component]
            spring = spr[component] - bonds_ref[...] * moved
            if turn == 0:
                if component == 0:
                    spring = spring + offset_ref[...]
                first[component] = spring
                moved = jnp.zeros_like(moved)
            else:
                spring = spring + first[component]
            drag = FRICTION * (beadflow[component] - speed)
            speed = speed + substep * alive * (SPRING * spring + drag)
            moved = moved + substep * alive * speed
            live_drag = alive * drag
            dragsum[component] = live_drag if turn == 0 else dragsum[component] + live_drag
            vel[component] = speed
            tab[component] = moved
        if turn + 1 < SUBSTEPS:
            send_ghosts(turn + 1)


def finish(passed, dragsum, moved_ref, vel, cell_ref, newpop_ref, disp_ref, newvel_ref, force_ref):
    cross, span = passed.shape[1:]
    rows = cell_ref.shape[0]
    halves = span // LANES

    chunk = 8
    packing = 16
    shift = span.bit_length() - 1
    iota = lax.broadcasted_iota(jnp.int32, (packing, LANES), 0).astype(F32)
    one, zero = jnp.ones((packing, LANES), BF16), jnp.zeros((packing, LANES), BF16)
    names = [(iota + float(q * packing)).astype(BF16) for q in range(max(span, cross) // packing)]

    def line(values, s):
        return jnp.broadcast_to(values[s : s + 1, :], (packing, LANES)).astype(BF16)

    def scatter(g, totals):
        at = pl.multiple_of(g * chunk, chunk)
        cell = cell_ref[pl.ds(at, chunk), :]
        cell_cross = (cell >> shift).astype(F32)
        cell_long = (cell & (span - 1)).astype(F32)
        pieces = []
        for component in range(3):
            drag = dragsum[component, pl.ds(at, chunk), :]
            head = drag.astype(BF16).astype(F32)
            pieces += [head, drag - head]
        place, weighted = [], []
        for s in range(chunk):
            row = line(cell_long, s)
            place.append(
                jnp.concatenate([jnp.where(names[q] == row, one, zero) for q in range(span // packing)], axis=0)
            )
            row = line(cell_cross, s)
            hits = [names[q] == row for q in range(cross // packing)]
            weighted.append(
                jnp.concatenate(
                    [jnp.where(hit, value, zero) for value in [line(p, s) for p in pieces] for hit in hits], axis=0
                )
            )
        return totals + lax.dot_general(
            jnp.concatenate(weighted, axis=1),
            jnp.concatenate(place, axis=1),
            (((1,), (1,)), ((), ())),
            preferred_element_type=F32,
        )

    summed = lax.fori_loop(0, rows // chunk, scatter, jnp.zeros((6 * cross, span), F32))
    for component in range(3):
        start = component * 2 * cross
        total = summed[start : start + cross] + summed[start + cross : start + 2 * cross]
        force_ref[component] = (-1.0 / SUBSTEPS) * total

    for component in range(3):
        for r in range(rows):
            at = slice(r * LANES, (r + 1) * LANES)
            disp_ref[component : component + 1, at] = moved_ref[component, r : r + 1, :]
            newvel_ref[component : component + 1, at] = vel[component, r : r + 1, :]

    factor = 1.0 - 0.5 / RELAX_TIME
    for block in range(cross // 8):
        at = slice(block * 8, block * 8 + 8)
        for half in range(halves):
            to = slice(half * LANES, (half + 1) * LANES)
            olds = [passed[member, at, to] for member in range(19)]
            rho = sum(olds[1:], olds[0])
            momentum = [
                sum(olds[m] for m in moving(c, 1)) - sum(olds[m] for m in moving(c, -1)) for c in range(3)
            ]
            force = [force_ref[component, at, to] for component in range(3)]
            inverse = 1.0 / rho
            flow = [(momentum[c] + 0.5 * force[c]) * inverse for c in range(3)]
            square = flow[0] * flow[0] + flow[1] * flow[1] + flow[2] * flow[2]
            flow_force = flow[0] * force[0] + flow[1] * force[1] + flow[2] * force[2]
            for member in range(19):
                weight = WEIGHTS[member]
                old = olds[member]
                along_flow = project(VELOCITIES[member], flow)
                force_along = project(VELOCITIES[member], force)
                if along_flow is None:
                    balance = weight * rho * (1.0 - 1.5 * square)
                    source = (factor * weight * 3.0) * (-flow_force)
                else:
                    balance = weight * rho * (
                        1.0 + along_flow * (3.0 + 4.5 * along_flow) - 1.5 * square
                    )
                    source = (factor * weight) * (
                        3.0 * (force_along - flow_force) + 9.0 * along_flow * force_along
                    )
                newpop_ref[member, at, to] = old - (old - balance) * (1.0 / RELAX_TIME) + source


def per_device(populations, positions, velocities, cells, partners, counts):
    cross, span = populations.shape[1:]
    capacity = positions.shape[1]
    rows = capacity // LANES
    nz, nx = lax.axis_size("gz"), lax.axis_size("xy")
    vmem = pl.BlockSpec(memory_space=pltpu.VMEM)
    cells = cells.reshape(rows, LANES)
    beads = jax.ShapeDtypeStruct((3, rows, LANES), F32)
    middle = pl.pallas_call(
        functools.partial(kernel, nz, nx),
        out_shape=(jax.ShapeDtypeStruct(populations.shape, F32), beads, beads, beads),
        in_specs=[vmem] * 5 + [pl.BlockSpec(memory_space=pltpu.SMEM)],
        out_specs=(vmem,) * 4,
        scratch_shapes=[
            pltpu.VMEM((2, rows, LANES), jnp.int32),
            pltpu.VMEM((2, rows, LANES), jnp.int32),
            pltpu.VMEM((2, 8, LANES), jnp.int32),
            pltpu.VMEM((2, 8, LANES), jnp.int32),
            pltpu.VMEM((3, rows, LANES), F32),
            pltpu.VMEM((8, LANES), jnp.int32),
            pltpu.VMEM((8, LANES), jnp.int32),
            pltpu.VMEM((3, rows, LANES), F32),
            pltpu.VMEM((rows, LANES), F32),
            pltpu.VMEM((2, rows, LANES), F32),
            pltpu.VMEM((2, rows, LANES), F32),
            pltpu.VMEM((2, cross, LANES), F32),
            pltpu.VMEM((2, cross, LANES), F32),
            pltpu.VMEM((2, 8, span), F32),
            pltpu.VMEM((2, 8, span), F32),
            pltpu.VMEM((SUBSTEPS, 3, 8, LANES), F32),
            pltpu.VMEM((SUBSTEPS, 2, 3, 8, LANES), F32),
            pltpu.VMEM((2, rows, LANES), jnp.int32),
            pltpu.VMEM((2, rows, LANES), jnp.int32),
            pltpu.VMEM((rows, LANES), F32),
            pltpu.VMEM((rows, LANES), F32),
            pltpu.VMEM((rows, LANES), F32),
            pltpu.VMEM((3, rows, LANES), F32),
            pltpu.VMEM((3, 8, LANES), F32),
            pltpu.VMEM((2, rows, LANES), jnp.int32),
            pltpu.VMEM((2, span // LANES, cross, LANES), jnp.int32),
            pltpu.SemaphoreType.DMA((6 + 2 * SUBSTEPS,)),
            pltpu.SemaphoreType.DMA((6 + 2 * SUBSTEPS,)),
        ],
        compiler_params=pltpu.CompilerParams(collective_id=0, has_side_effects=True),
    )(populations, positions, velocities, cells, partners, counts)
    return pl.pallas_call(
        finish,
        out_shape=(
            jax.ShapeDtypeStruct(populations.shape, F32),
            jax.ShapeDtypeStruct(positions.shape, F32),
            jax.ShapeDtypeStruct(velocities.shape, F32),
        ),
        in_specs=[vmem] * 5,
        out_specs=(vmem,) * 3,
        scratch_shapes=[pltpu.VMEM((3, cross, span), F32)],
    )(*middle, cells)


def solution(mesh):
    in_specs = (
        P(None, "xy", "gz"),
        P(None, ("gz", "xy")),
        P(None, ("gz", "xy")),
        P(("gz", "xy")),
        P(None, ("gz", "xy")),
        P(("gz", "xy")),
    )
    out_specs = (P(None, "xy", "gz"), P(None, ("gz", "xy")), P(None, ("gz", "xy")))
    return jax.shard_map(
        per_device, mesh=mesh, in_specs=in_specs, out_specs=out_specs, check_vma=False
    )
```

profile of v0, /device:TPU:0, one launch (start us, length us, event | category | flops | bytes accessed | tf_op | source)
XLA Modules:
  0.0 31.8 jit_solution(7383774894193213546)
XLA Ops:
  1.3 25.1 %shard_map.85 = (f32[19,32,256]{2,1,0:T(8,128)}, f32[3,64,128]{2,1,0:T(8,128)}, f32[3,64,128]{2,1,0:T(8,128)}, f32[3,64,128]{2,1,0:T(8,128)}) custom-call(f32[19,32,256]{2,1,0:T(8,128)} %pop_ref.1, f32[3,8192]{1,0:T(4,128)} %pos_ref.1, f32[3,8192]{1,0:T(4,128)} %vel_ref.1, s32[64,128]{1,0:T(8,128)} %bitcast.1, s32[2,8192]{1,0:T(2,128)} %part_ref.1, ...), custom_call_target="tpu_custom_call" | custom-call | tf_op jit(solution)/shard_map/pallas_call | solution.py:559
  26.4 5.4 %shard_map.86 = (f32[19,32,256]{2,1,0:T(8,128)}, f32[3,8192]{1,0:T(4,128)}, f32[3,8192]{1,0:T(4,128)}) custom-call(f32[19,32,256]{2,1,0:T(8,128)} %get-tuple-element.7.passed, f32[3,64,128]{2,1,0:T(8,128)} %get-tuple-element.8.dragsum, f32[3,64,128]{2,1,0:T(8,128)} %get-tuple-element.9.moved_ref, f32[3,64,128]{2,1,0:T(8,128)} %get-tuple-element.10.vel, ...), custom_call_target="tpu_custom_call" | custom-call | tf_op jit(solution)/shard_map/pallas_call | solution.py:596
where the time goes:
time: 32 us; the launch traced here: 31.8 us
  Pallas kernels  30.5 us (95%)
  between operations  1.29 us (4%)
    pallas_call x1, Pallas kernels, per_device(): pl.pallas_call(functools.partial(kernel, nz, nx), out_shape=(jax.ShapeDty...  25.1 us
    pallas_call x1, Pallas kernels, per_device(): pl.pallas_call(finish, out_shape=(jax.ShapeDtypeStruct(populations.shape,...  5.39 us

commit v1 on v0

--- a/solution.py
+++ b/solution.py
@@ -99,9 +99,11 @@
     part_ref,
     count_ref,
     passed,
-    dragsum,
+    force_ref,
     tab,
     vel,
+    dragsum,
+    summed,
     hi_ref,
     lo_ref,
     ghi_ref,
@@ -263,15 +265,20 @@
         copies["g0", turn].start()
         copies["g1", turn].start()
 
-    def own_springs(turn):
+    def pack_words(turn):
         scale, base = (START_SCALE, 0.0) if turn == 0 else (MOVE_SCALE, MOVE_BASE)
         words = pack([tab[component] for component in range(3)], scale, base)
         words_ref[0] = words[0]
         words_ref[1] = words[1]
 
-        @pl.loop(0, rows // 8)
+    def own_springs(turn, begin, end, beside=None):
+        scale, base = (START_SCALE, 0.0) if turn == 0 else (MOVE_SCALE, MOVE_BASE)
+
+        @pl.loop(begin, end)
         def _(g):
             at = pl.multiple_of(g * 8, 8)
+            if beside is not None:
+                beside(at)
             totals = None
             for column in range(2):
                 found = unpack(
@@ -323,7 +330,9 @@
         ghi_ref[column] = listed[column]
 
     send_ghosts(0)
-    own_springs(0)
+    groups = rows // 8
+    pack_words(0)
+    own_springs(0, 0, groups // 2)
 
     copies["z0"].wait()
     copies["z1"].wait()
@@ -356,6 +365,8 @@
             wsend[side, k : k + 1, :] = value[cross - 1 :, :] if sign > 0 else value[:1, :]
     copies["w0"].start()
     copies["w1"].start()
+
+    own_springs(0, groups // 2, groups)
 
     copies["r0"].wait()
     copies["r1"].wait()
@@ -432,7 +443,16 @@
     substep = 1.0 / SUBSTEPS
     for turn in range(SUBSTEPS):
         if turn > 0:
-            own_springs(turn)
+            pack_words(turn)
+            last = turn + 1 == SUBSTEPS
+            if last:
+                summed[...] = jnp.zeros(summed.shape, F32)
+            own_springs(turn, 0, groups, functools.partial(scatter, cell_ref, dragsum, summed) if last else None)
+            if last:
+                for component in range(3):
+                    begin = component * 2 * cross
+                    total = summed[begin : begin + cross, :] + summed[begin + cross : begin + 2 * cross, :]
+                    force_ref[component] = (-1.0 / SUBSTEPS) * total
         copies["g0", turn].wait()
         copies["g1", turn].wait()
         ghost_springs(turn)
@@ -450,19 +470,20 @@
             drag = FRICTION * (beadflow[component] - speed)
             speed = speed + substep * alive * (SPRING * spring + drag)
             moved = moved + substep * alive * speed
-            live_drag = alive * drag
-            dragsum[component] = live_drag if turn == 0 else dragsum[component] + live_drag
+            if turn == 0:
+                dragsum[component] = alive * drag
+            elif turn + 1 < SUBSTEPS:
+                dragsum[component] = dragsum[component] + alive * drag
+            if turn + 2 == SUBSTEPS:
+                dragsum[component] = dragsum[component] + alive * (FRICTION * (beadflow[component] - speed))
             vel[component] = speed
             tab[component] = moved
         if turn + 1 < SUBSTEPS:
             send_ghosts(turn + 1)
 
 
-def finish(passed, dragsum, moved_ref, vel, cell_ref, newpop_ref, disp_ref, newvel_ref, force_ref):
-    cross, span = passed.shape[1:]
-    rows = cell_ref.shape[0]
-    halves = span // LANES
-
+def scatter(cell_ref, dragsum, summed, at):
+    cross, span = summed.shape[0] // 6, summed.shape[1]
     chunk = 8
     packing = 16
     shift = span.bit_length() - 1
@@ -473,41 +494,39 @@
     def line(values, s):
         return jnp.broadcast_to(values[s : s + 1, :], (packing, LANES)).astype(BF16)
 
-    def scatter(g, totals):
-        at = pl.multiple_of(g * chunk, chunk)
-        cell = cell_ref[pl.ds(at, chunk), :]
-        cell_cross = (cell >> shift).astype(F32)
-        cell_long = (cell & (span - 1)).astype(F32)
-        pieces = []
-        for component in range(3):
-            drag = dragsum[component, pl.ds(at, chunk), :]
-            head = drag.astype(BF16).astype(F32)
-            pieces += [head, drag - head]
-        place, weighted = [], []
-        for s in range(chunk):
-            row = line(cell_long, s)
-            place.append(
-                jnp.concatenate([jnp.where(names[q] == row, one, zero) for q in range(span // packing)], axis=0)
+    cell = cell_ref[pl.ds(at, chunk), :]
+    cell_cross = (cell >> shift).astype(F32)
+    cell_long = (cell & (span - 1)).astype(F32)
+    pieces = []
+    for component in range(3):
+        drag = dragsum[component, pl.ds(at, chunk), :]
+        head = drag.astype(BF16).astype(F32)
+        pieces += [head, drag - head]
+    place, weighted = [], []
+    for s in range(chunk):
+        row = line(cell_long, s)
+        place.append(
+            jnp.concatenate([jnp.where(names[q] == row, one, zero) for q in range(span // packing)], axis=0)
+        )
+        row = line(cell_cross, s)
+        hits = [names[q] == row for q in range(cross // packing)]
+        weighted.append(
+            jnp.concatenate(
+                [jnp.where(hit, value, zero) for value in [line(p, s) for p in pieces] for hit in hits], axis=0
             )
-            row = line(cell_cross, s)
-            hits = [names[q] == row for q in range(cross // packing)]
-            weighted.append(
-                jnp.concatenate(
-                    [jnp.where(hit, value, zero) for value in [line(p, s) for p in pieces] for hit in hits], axis=0
-                )
-            )
-        return totals + lax.dot_general(
-            jnp.concatenate(weighted, axis=1),
-            jnp.concatenate(place, axis=1),
-            (((1,), (1,)), ((), ())),
-            preferred_element_type=F32,
         )
-
-    summed = lax.fori_loop(0, rows // chunk, scatter, jnp.zeros((6 * cross, span), F32))
-    for component in range(3):
-        start = component * 2 * cross
-        total = summed[start : start + cross] + summed[start + cross : start + 2 * cross]
-        force_ref[component] = (-1.0 / SUBSTEPS) * total
+    summed[...] += lax.dot_general(
+        jnp.concatenate(weighted, axis=1),
+        jnp.concatenate(place, axis=1),
+        (((1,), (1,)), ((), ())),
+        preferred_element_type=F32,
+    )
+
+
+def finish(passed, force_ref, moved_ref, vel, newpop_ref, disp_ref, newvel_ref):
+    cross, span = passed.shape[1:]
+    rows = vel.shape[1]
+    halves = span // LANES
 
     for component in range(3):
         for r in range(rows):
@@ -558,10 +577,17 @@
     beads = jax.ShapeDtypeStruct((3, rows, LANES), F32)
     middle = pl.pallas_call(
         functools.partial(kernel, nz, nx),
-        out_shape=(jax.ShapeDtypeStruct(populations.shape, F32), beads, beads, beads),
+        out_shape=(
+            jax.ShapeDtypeStruct(populations.shape, F32),
+            jax.ShapeDtypeStruct((3, cross, span), F32),
+            beads,
+            beads,
+        ),
         in_specs=[vmem] * 5 + [pl.BlockSpec(memory_space=pltpu.SMEM)],
         out_specs=(vmem,) * 4,
         scratch_shapes=[
+            pltpu.VMEM((3, rows, LANES), F32),
+            pltpu.VMEM((6 * cross, span), F32),
             pltpu.VMEM((2, rows, LANES), jnp.int32),
             pltpu.VMEM((2, rows, LANES), jnp.int32),
             pltpu.VMEM((2, 8, LANES), jnp.int32),
@@ -600,10 +626,9 @@
             jax.ShapeDtypeStruct(positions.shape, F32),
             jax.ShapeDtypeStruct(velocities.shape, F32),
         ),
-        in_specs=[vmem] * 5,
+        in_specs=[vmem] * 4,
         out_specs=(vmem,) * 3,
-        scratch_shapes=[pltpu.VMEM((3, cross, span), F32)],
-    )(*middle, cells)
+    )(*middle)
 
 
 def solution(mesh):

time: 32 us -> 28.4 us (0.89)
  Pallas kernels: 30.5 us -> 26.9 us
    pallas_call x1, Pallas kernels: 5.39 us -> 2.58 us  [per_device(): pl.pallas_call(finish, out_shape=(jax.ShapeDtypeStruct(populations.shape,...]
    pallas_call x1, Pallas kernels: 25.1 us -> 24.3 us  [per_device(): pl.pallas_call(functools.partial(kernel, nz, nx), out_shape=(jax.ShapeDty...]
where the time goes in v1:
time: 28.4 us; the launch traced here: 28.2 us
  Pallas kernels  26.9 us (95%)
  between operations  1.29 us (5%)
    pallas_call x1, Pallas kernels, per_device(): pl.pallas_call(functools.partial(kernel, nz, nx), out_shape=(jax.ShapeDty...  24.3 us
    pallas_call x1, Pallas kernels, per_device(): pl.pallas_call(finish, out_shape=(jax.ShapeDtypeStruct(populations.shape,...  2.58 us

profile of v1, /device:TPU:0, one launch (start us, length us, event | category | flops | bytes accessed | tf_op | source)
XLA Modules:
  0.0 28.2 jit_solution(900327178325869955)
XLA Ops:
  1.3 24.3 %shard_map.85 = (f32[19,32,256]{2,1,0:T(8,128)}, f32[3,32,256]{2,1,0:T(8,128)}, f32[3,64,128]{2,1,0:T(8,128)}, f32[3,64,128]{2,1,0:T(8,128)}) custom-call(f32[19,32,256]{2,1,0:T(8,128)} %pop_ref.1, f32[3,8192]{1,0:T(4,128)} %pos_ref.1, f32[3,8192]{1,0:T(4,128)} %vel_ref.1, s32[64,128]{1,0:T(8,128)} %bitcast.1, s32[2,8192]{1,0:T(2,128)} %part_ref.1, ...), custom_call_target="tpu_custom_call" | custom-call | tf_op jit(solution)/shard_map/pallas_call | solution.py:578
  25.6 2.6 %shard_map.86 = (f32[19,32,256]{2,1,0:T(8,128)}, f32[3,8192]{1,0:T(4,128)}, f32[3,8192]{1,0:T(4,128)}) custom-call(f32[19,32,256]{2,1,0:T(8,128)} %get-tuple-element.7.passed, f32[3,32,256]{2,1,0:T(8,128)} %get-tuple-element.8.force_ref, f32[3,64,128]{2,1,0:T(8,128)} %get-tuple-element.9.moved_ref, f32[3,64,128]{2,1,0:T(8,128)} %get-tuple-element.10.vel), custom_call_target="tpu_custom_call" | custom-call | tf_op jit(solution)/shard_map/pallas_call | solution.py:622

commit v2 on v1

--- a/solution.py
+++ b/solution.py
@@ -40,8 +40,8 @@
 SPRING = 1.0
 FRICTION = 0.25
 START_SCALE = 2.0**16
-MOVE_SCALE = 2.0**15
-MOVE_BASE = 32.0
+MOVE_TOP = 2.0**15 - 2.0
+SMALLEST = 1e-30
 FLOW_SCALE = 2.0**19
 FLOW_BASE = 2.0
 
@@ -104,6 +104,7 @@
     vel,
     dragsum,
     summed,
+    step_ref,
     hi_ref,
     lo_ref,
     ghi_ref,
@@ -136,6 +137,7 @@
     cross, span = pop_ref.shape[1], pop_ref.shape[2]
     capacity = pos_ref.shape[1]
     rows = capacity // LANES
+    groups = rows // 8
     me_z, me_x = lax.axis_index("gz"), lax.axis_index("xy")
     up = {"gz": lax.rem(me_z + 1, nz)}
     down = {"gz": lax.rem(me_z + nz - 1, nz)}
@@ -266,19 +268,23 @@
         copies["g1", turn].start()
 
     def pack_words(turn):
-        scale, base = (START_SCALE, 0.0) if turn == 0 else (MOVE_SCALE, MOVE_BASE)
-        words = pack([tab[component] for component in range(3)], scale, base)
-        words_ref[0] = words[0]
-        words_ref[1] = words[1]
-
-    def own_springs(turn, begin, end, beside=None):
-        scale, base = (START_SCALE, 0.0) if turn == 0 else (MOVE_SCALE, MOVE_BASE)
-
+        if turn == 0:
+            words = pack([tab[component] for component in range(3)], START_SCALE, 0.0)
+            words_ref[0] = words[0]
+            words_ref[1] = words[1]
+            return
+        far = jnp.maximum(jnp.maximum(jnp.abs(tab[0]), jnp.abs(tab[1])), jnp.abs(tab[2]))
+        far = jnp.maximum(jnp.max(far, axis=(0, 1), keepdims=True), SMALLEST)
+        step_ref[...] = jnp.broadcast_to(far * (1.0 / MOVE_TOP), (8, LANES))
+        scale = MOVE_TOP / far
+        fixed = [(tab[component] * scale + (MOVE_TOP + 1.5)).astype(jnp.int32) for component in range(3)]
+        words_ref[0] = (fixed[0] << 16) | fixed[1]
+        words_ref[1, : rows // 2, :] = (fixed[2][: rows // 2] << 16) | fixed[2][rows // 2 :]
+
+    def start_springs(begin, end):
         @pl.loop(begin, end)
         def _(g):
             at = pl.multiple_of(g * 8, 8)
-            if beside is not None:
-                beside(at)
             totals = None
             for column in range(2):
                 found = unpack(
@@ -288,8 +294,30 @@
             count = inner[pl.ds(at, 8), :]
             for component in range(3):
                 value = totals[component].astype(F32)
-                value = (value + 0.5 * count) * (1.0 / scale) if turn == 0 else value * (1.0 / scale) - base * count
-                spr[component, pl.ds(at, 8), :] = value
+                spr[component, pl.ds(at, 8), :] = (value + 0.5 * count) * (1.0 / START_SCALE)
+
+    def moved_springs(beside=None):
+        @pl.loop(0, groups)
+        def _(g):
+            at = pl.multiple_of(g * 8, 8)
+            if beside is not None:
+                beside(at)
+            totals = None
+            for column in range(2):
+                hi, lo = hi_ref[column, pl.ds(at, 8), :], lo_ref[column, pl.ds(at, 8), :]
+                half = rows // 2
+                folded = jnp.where(hi >= half, hi - half, hi)
+                pair = sweep(packed_row, hi, lo, 1)[0]
+                third = sweep(lambda _, r: packed_row(1, r), folded, lo, 1, half)[0]
+                found = (
+                    lax.shift_right_logical(pair, 16),
+                    pair & 65535,
+                    jnp.where(hi >= half, third & 65535, lax.shift_right_logical(third, 16)),
+                )
+                totals = found if totals is None else [x + y for x, y in zip(totals, found)]
+            base = inner[pl.ds(at, 8), :] * (MOVE_TOP + 1.0)
+            for component in range(3):
+                spr[component, pl.ds(at, 8), :] = (totals[component].astype(F32) - base) * step_ref[...]
 
     def ghost_springs(turn):
         near = []
@@ -330,9 +358,8 @@
         ghi_ref[column] = listed[column]
 
     send_ghosts(0)
-    groups = rows // 8
     pack_words(0)
-    own_springs(0, 0, groups // 2)
+    start_springs(0, groups // 2)
 
     copies["z0"].wait()
     copies["z1"].wait()
@@ -366,7 +393,7 @@
     copies["w0"].start()
     copies["w1"].start()
 
-    own_springs(0, groups // 2, groups)
+    start_springs(groups // 2, groups)
 
     copies["r0"].wait()
     copies["r1"].wait()
@@ -447,7 +474,7 @@
             last = turn + 1 == SUBSTEPS
             if last:
                 summed[...] = jnp.zeros(summed.shape, F32)
-            own_springs(turn, 0, groups, functools.partial(scatter, cell_ref, dragsum, summed) if last else None)
+            moved_springs(functools.partial(scatter, cell_ref, dragsum, summed) if last else None)
             if last:
                 for component in range(3):
                     begin = component * 2 * cross
@@ -515,11 +542,14 @@
                 [jnp.where(hit, value, zero) for value in [line(p, s) for p in pieces] for hit in hits], axis=0
             )
         )
-    summed[...] += lax.dot_general(
-        jnp.concatenate(weighted, axis=1),
-        jnp.concatenate(place, axis=1),
-        (((1,), (1,)), ((), ())),
-        preferred_element_type=F32,
+    summed[...] += sum(
+        lax.dot_general(
+            jnp.concatenate(weighted[k : k + 2], axis=1),
+            jnp.concatenate(place[k : k + 2], axis=1),
+            (((1,), (1,)), ((), ())),
+            preferred_element_type=F32,
+        )
+        for k in range(0, chunk, 2)
     )
 
 
@@ -588,6 +618,7 @@
         scratch_shapes=[
             pltpu.VMEM((3, rows, LANES), F32),
             pltpu.VMEM((6 * cross, span), F32),
+            pltpu.VMEM((8, LANES), F32),
             pltpu.VMEM((2, rows, LANES), jnp.int32),
             pltpu.VMEM((2, rows, LANES), jnp.int32),
             pltpu.VMEM((2, 8, LANES), jnp.int32),

time: 28.4 us -> 27.7 us (0.975)
  Pallas kernels: 26.9 us -> 26.3 us
    pallas_call x1, Pallas kernels: 24.3 us -> 23.7 us  [per_device(): pl.pallas_call(functools.partial(kernel, nz, nx), out_shape=(jax.ShapeDty...]
where the time goes in v2:
time: 27.7 us; the launch traced here: 27.6 us
  Pallas kernels  26.3 us (95%)
  between operations  1.29 us (5%)
    pallas_call x1, Pallas kernels, per_device(): pl.pallas_call(functools.partial(kernel, nz, nx), out_shape=(jax.ShapeDty...  23.7 us
    pallas_call x1, Pallas kernels, per_device(): pl.pallas_call(finish, out_shape=(jax.ShapeDtypeStruct(populations.shape,...  2.58 us

profile of v2, /device:TPU:0, one launch (start us, length us, event | category | flops | bytes accessed | tf_op | source)
XLA Modules:
  0.0 27.6 jit_solution(4775572147880024436)
XLA Ops:
  1.3 23.7 %shard_map.85 = (f32[19,32,256]{2,1,0:T(8,128)}, f32[3,32,256]{2,1,0:T(8,128)}, f32[3,64,128]{2,1,0:T(8,128)}, f32[3,64,128]{2,1,0:T(8,128)}) custom-call(f32[19,32,256]{2,1,0:T(8,128)} %pop_ref.1, f32[3,8192]{1,0:T(4,128)} %pos_ref.1, f32[3,8192]{1,0:T(4,128)} %vel_ref.1, s32[64,128]{1,0:T(8,128)} %bitcast.1, s32[2,8192]{1,0:T(2,128)} %part_ref.1, ...), custom_call_target="tpu_custom_call" | custom-call | tf_op jit(solution)/shard_map/pallas_call | solution.py:608
  25.0 2.6 %shard_map.86 = (f32[19,32,256]{2,1,0:T(8,128)}, f32[3,8192]{1,0:T(4,128)}, f32[3,8192]{1,0:T(4,128)}) custom-call(f32[19,32,256]{2,1,0:T(8,128)} %get-tuple-element.7.passed, f32[3,32,256]{2,1,0:T(8,128)} %get-tuple-element.8.force_ref, f32[3,64,128]{2,1,0:T(8,128)} %get-tuple-element.9.moved_ref, f32[3,64,128]{2,1,0:T(8,128)} %get-tuple-element.10.vel), custom_call_target="tpu_custom_call" | custom-call | tf_op jit(solution)/shard_map/pallas_call | solution.py:653

commit v3 on v2

--- a/solution.py
+++ b/solution.py
@@ -98,10 +98,12 @@
     cell_ref,
     part_ref,
     count_ref,
-    passed,
+    passed_out,
     force_ref,
     tab,
     vel,
+    passed,
+    out_sem,
     dragsum,
     summed,
     step_ref,
@@ -440,6 +442,8 @@
             if VELOCITIES[member][component] != 0:
                 term = value if VELOCITIES[member][component] > 0 else -value
                 momentum[component] = term if momentum[component] is None else momentum[component] + term
+    leaving = pltpu.make_async_copy(passed, passed_out, out_sem)
+    leaving.start()
     inverse = 1.0 / density
     words = pack([momentum[component] * inverse for component in range(3)], FLOW_SCALE, FLOW_BASE)
     for half in range(span // LANES):
@@ -507,6 +511,7 @@
             tab[component] = moved
         if turn + 1 < SUBSTEPS:
             send_ghosts(turn + 1)
+    leaving.wait()
 
 
 def scatter(cell_ref, dragsum, summed, at):
@@ -553,19 +558,55 @@
     )
 
 
-def finish(passed, force_ref, moved_ref, vel, newpop_ref, disp_ref, newvel_ref):
+def finish(
+    passed_in,
+    force_in,
+    moved_in,
+    vel_in,
+    newpop_out,
+    disp_out,
+    newvel_out,
+    passed,
+    force_ref,
+    moved_ref,
+    vel,
+    newpop_ref,
+    disp_ref,
+    newvel_ref,
+    in_sems,
+    out_sems,
+):
     cross, span = passed.shape[1:]
     rows = vel.shape[1]
     halves = span // LANES
-
-    for component in range(3):
-        for r in range(rows):
-            at = slice(r * LANES, (r + 1) * LANES)
-            disp_ref[component : component + 1, at] = moved_ref[component, r : r + 1, :]
-            newvel_ref[component : component + 1, at] = vel[component, r : r + 1, :]
+    blocks = cross // 8
+
+    def rows_of(ref, block):
+        return ref.at[:, pl.ds(block * 8, 8), :]
+
+    beads_in = [(moved_in, moved_ref), (vel_in, vel), (force_in, force_ref)]
+    coming = [pltpu.make_async_copy(a, b, in_sems.at[blocks + k]) for k, (a, b) in enumerate(beads_in)]
+    parts = [
+        pltpu.make_async_copy(rows_of(passed_in, b), rows_of(passed, b), in_sems.at[b]) for b in range(blocks)
+    ]
+    for each in coming + parts:
+        each.start()
+    going = [
+        pltpu.make_async_copy(rows_of(newpop_ref, b), rows_of(newpop_out, b), out_sems.at[b])
+        for b in range(blocks)
+    ]
+    for k, (held, target, result) in enumerate(((moved_ref, disp_ref, disp_out), (vel, newvel_ref, newvel_out))):
+        coming[k].wait()
+        for component in range(3):
+            for r in range(rows):
+                target[component : component + 1, r * LANES : (r + 1) * LANES] = held[component, r : r + 1, :]
+        going.append(pltpu.make_async_copy(target, result, out_sems.at[blocks + k]))
+        going[-1].start()
+    coming[2].wait()
 
     factor = 1.0 - 0.5 / RELAX_TIME
-    for block in range(cross // 8):
+    for block in range(blocks):
+        parts[block].wait()
         at = slice(block * 8, block * 8 + 8)
         for half in range(halves):
             to = slice(half * LANES, (half + 1) * LANES)
@@ -595,6 +636,9 @@
                         3.0 * (force_along - flow_force) + 9.0 * along_flow * force_along
                     )
                 newpop_ref[member, at, to] = old - (old - balance) * (1.0 / RELAX_TIME) + source
+        going[block].start()
+    for each in going:
+        each.wait()
 
 
 def per_device(populations, positions, velocities, cells, partners, counts):
@@ -603,6 +647,7 @@
     rows = capacity // LANES
     nz, nx = lax.axis_size("gz"), lax.axis_size("xy")
     vmem = pl.BlockSpec(memory_space=pltpu.VMEM)
+    anywhere = pl.BlockSpec(memory_space=pl.ANY)
     cells = cells.reshape(rows, LANES)
     beads = jax.ShapeDtypeStruct((3, rows, LANES), F32)
     middle = pl.pallas_call(
@@ -614,8 +659,10 @@
             beads,
         ),
         in_specs=[vmem] * 5 + [pl.BlockSpec(memory_space=pltpu.SMEM)],
-        out_specs=(vmem,) * 4,
+        out_specs=(anywhere, vmem, vmem, vmem),
         scratch_shapes=[
+            pltpu.VMEM(populations.shape, F32),
+            pltpu.SemaphoreType.DMA,
             pltpu.VMEM((3, rows, LANES), F32),
             pltpu.VMEM((6 * cross, span), F32),
             pltpu.VMEM((8, LANES), F32),
@@ -657,8 +704,19 @@
             jax.ShapeDtypeStruct(positions.shape, F32),
             jax.ShapeDtypeStruct(velocities.shape, F32),
         ),
-        in_specs=[vmem] * 4,
-        out_specs=(vmem,) * 3,
+        in_specs=[anywhere] * 4,
+        out_specs=(anywhere,) * 3,
+        scratch_shapes=[
+            pltpu.VMEM(populations.shape, F32),
+            pltpu.VMEM((3, cross, span), F32),
+            pltpu.VMEM((3, rows, LANES), F32),
+            pltpu.VMEM((3, rows, LANES), F32),
+            pltpu.VMEM(populations.shape, F32),
+            pltpu.VMEM(positions.shape, F32),
+            pltpu.VMEM(velocities.shape, F32),
+            pltpu.SemaphoreType.DMA((cross // 8 + 3,)),
+            pltpu.SemaphoreType.DMA((cross // 8 + 2,)),
+        ],
     )(*middle)
 
 

time: 27.7 us -> 27.4 us (0.989)
  Pallas kernels: 26.3 us -> 25.9 us
where the time goes in v3:
time: 27.4 us; the launch traced here: 27.2 us
  Pallas kernels  25.9 us (95%)
  between operations  1.29 us (5%)
    pallas_call x1, Pallas kernels, per_device(): pl.pallas_call(functools.partial(kernel, nz, nx), out_shape=(jax.ShapeDty...  23.6 us
    pallas_call x1, Pallas kernels, per_device(): pl.pallas_call(finish, out_shape=(jax.ShapeDtypeStruct(populations.shape,...  2.35 us

profile of v3, /device:TPU:0, one launch (start us, length us, event | category | flops | bytes accessed | tf_op | source)
XLA Modules:
  0.0 27.2 jit_solution(16921215331700540028)
XLA Ops:
  1.3 23.6 %shard_map.85 = (f32[19,32,256]{2,1,0:T(8,128)}, f32[3,32,256]{2,1,0:T(8,128)}, f32[3,64,128]{2,1,0:T(8,128)}, f32[3,64,128]{2,1,0:T(8,128)}) custom-call(f32[19,32,256]{2,1,0:T(8,128)} %pop_ref.1, f32[3,8192]{1,0:T(4,128)} %pos_ref.1, f32[3,8192]{1,0:T(4,128)} %vel_ref.1, s32[64,128]{1,0:T(8,128)} %bitcast.1, s32[2,8192]{1,0:T(2,128)} %part_ref.1, ...), custom_call_target="tpu_custom_call" | custom-call | tf_op jit(solution)/shard_map/pallas_call | solution.py:653
  24.9 2.3 %shard_map.86 = (f32[19,32,256]{2,1,0:T(8,128)}, f32[3,8192]{1,0:T(4,128)}, f32[3,8192]{1,0:T(4,128)}) custom-call(f32[19,32,256]{2,1,0:T(8,128)} %get-tuple-element.7.passed_in, f32[3,32,256]{2,1,0:T(8,128)} %get-tuple-element.8.force_in, f32[3,64,128]{2,1,0:T(8,128)} %get-tuple-element.9.moved_in, f32[3,64,128]{2,1,0:T(8,128)} %get-tuple-element.10.vel_in), custom_call_target="tpu_custom_call" | custom-call | tf_op jit(solution)/shard_map/pallas_call | solution.py:700

commit v4 on v3

--- a/solution.py
+++ b/solution.py
@@ -42,8 +42,6 @@
 START_SCALE = 2.0**16
 MOVE_TOP = 2.0**15 - 2.0
 SMALLEST = 1e-30
-FLOW_SCALE = 2.0**19
-FLOW_BASE = 2.0
 
 MESH = pl.DeviceIdType.MESH
 F32 = jnp.float32
@@ -71,13 +69,9 @@
     return jnp.broadcast_to(row, (8, LANES))
 
 
-def pack(values, scale, base):
+def pack(values, scale):
     top = float(2**21 - 1)
-    fixed = [
-        jnp.clip((v + base) * scale, 0.0, top).astype(jnp.int32) if base == 0.0
-        else jnp.clip((v + base) * scale + 0.5, 0.0, top).astype(jnp.int32)
-        for v in values
-    ]
+    fixed = [jnp.clip(v * scale, 0.0, top).astype(jnp.int32) for v in values]
     return (fixed[0] << 11) | (fixed[2] >> 10), (fixed[1] << 11) | (fixed[2] & 1023)
 
 
@@ -269,17 +263,30 @@
         copies["g0", turn].start()
         copies["g1", turn].start()
 
+    def sixteen(values):
+        far = jnp.maximum(jnp.maximum(jnp.abs(values[0]), jnp.abs(values[1])), jnp.abs(values[2]))
+        far = jnp.maximum(jnp.max(far, axis=(0, 1), keepdims=True), SMALLEST)
+        step_ref[...] = jnp.broadcast_to(far * (1.0 / MOVE_TOP), (8, LANES))
+        scale = MOVE_TOP / far
+        return [(v * scale + (MOVE_TOP + 1.5)).astype(jnp.int32) for v in values]
+
+    def sweep_folded(source, hi, lo, lines):
+        half = lines // 2
+        pair = sweep(source, hi, lo, 1, lines)[0]
+        third = sweep(lambda _, r: source(1, r), jnp.where(hi >= half, hi - half, hi), lo, 1, half)[0]
+        return (
+            lax.shift_right_logical(pair, 16),
+            pair & 65535,
+            jnp.where(hi >= half, third & 65535, lax.shift_right_logical(third, 16)),
+        )
+
     def pack_words(turn):
         if turn == 0:
-            words = pack([tab[component] for component in range(3)], START_SCALE, 0.0)
+            words = pack([tab[component] for component in range(3)], START_SCALE)
             words_ref[0] = words[0]
             words_ref[1] = words[1]
             return
-        far = jnp.maximum(jnp.maximum(jnp.abs(tab[0]), jnp.abs(tab[1])), jnp.abs(tab[2]))
-        far = jnp.maximum(jnp.max(far, axis=(0, 1), keepdims=True), SMALLEST)
-        step_ref[...] = jnp.broadcast_to(far * (1.0 / MOVE_TOP), (8, LANES))
-        scale = MOVE_TOP / far
-        fixed = [(tab[component] * scale + (MOVE_TOP + 1.5)).astype(jnp.int32) for component in range(3)]
+        fixed = sixteen([tab[component] for component in range(3)])
         words_ref[0] = (fixed[0] << 16) | fixed[1]
         words_ref[1, : rows // 2, :] = (fixed[2][: rows // 2] << 16) | fixed[2][rows // 2 :]
 
@@ -307,15 +314,7 @@
             totals = None
             for column in range(2):
                 hi, lo = hi_ref[column, pl.ds(at, 8), :], lo_ref[column, pl.ds(at, 8), :]
-                half = rows // 2
-                folded = jnp.where(hi >= half, hi - half, hi)
-                pair = sweep(packed_row, hi, lo, 1)[0]
-                third = sweep(lambda _, r: packed_row(1, r), folded, lo, 1, half)[0]
-                found = (
-                    lax.shift_right_logical(pair, 16),
-                    pair & 65535,
-                    jnp.where(hi >= half, third & 65535, lax.shift_right_logical(third, 16)),
-                )
+                found = sweep_folded(packed_row, hi, lo, rows)
                 totals = found if totals is None else [x + y for x, y in zip(totals, found)]
             base = inner[pl.ds(at, 8), :] * (MOVE_TOP + 1.0)
             for component in range(3):
@@ -445,10 +444,12 @@
     leaving = pltpu.make_async_copy(passed, passed_out, out_sem)
     leaving.start()
     inverse = 1.0 / density
-    words = pack([momentum[component] * inverse for component in range(3)], FLOW_SCALE, FLOW_BASE)
+    fixed = sixteen([momentum[component] * inverse for component in range(3)])
+    both = (fixed[0] << 16) | fixed[1]
+    folded = (fixed[2][: cross // 2] << 16) | fixed[2][cross // 2 :]
     for half in range(span // LANES):
-        for word in range(2):
-            flow_words[word, half] = words[word][:, half * LANES : (half + 1) * LANES]
+        flow_words[0, half] = both[:, half * LANES : (half + 1) * LANES]
+        flow_words[1, half, : cross // 2, :] = folded[:, half * LANES : (half + 1) * LANES]
 
     halves = span // LANES
 
@@ -460,11 +461,11 @@
     def _(g):
         at = pl.multiple_of(g * 8, 8)
         cell = cell_ref[pl.ds(at, 8), :]
-        found = unpack(*sweep(flow_row, cell >> 7, cell & (LANES - 1), 2, cross * halves))
+        found = sweep_folded(flow_row, cell >> 7, cell & (LANES - 1), cross * halves)
         for component in range(3):
             beadflow[component, pl.ds(at, 8), :] = (
-                found[component].astype(F32) * (1.0 / FLOW_SCALE) - FLOW_BASE
-            )
+                found[component].astype(F32) - (MOVE_TOP + 1.0)
+            ) * step_ref[...]
 
     slot_index = (
         lax.broadcasted_iota(jnp.int32, (rows, LANES), 0) * LANES

time: 27.4 us -> 27.2 us (level)
  no operation moved by 1% of the time
where the time goes in v4:
time: 27.2 us; the launch traced here: 27 us
  Pallas kernels  25.7 us (94%)
  between operations  1.29 us (5%)
    pallas_call x1, Pallas kernels, per_device(): pl.pallas_call(functools.partial(kernel, nz, nx), out_shape=(jax.ShapeDty...  23.4 us
    pallas_call x1, Pallas kernels, per_device(): pl.pallas_call(finish, out_shape=(jax.ShapeDtypeStruct(populations.shape,...  2.35 us

profile of v4, /device:TPU:0, one launch (start us, length us, event | category | flops | bytes accessed | tf_op | source)
XLA Modules:
  0.0 27.0 jit_solution(3589268810935497135)
XLA Ops:
  1.3 23.4 %shard_map.85 = (f32[19,32,256]{2,1,0:T(8,128)}, f32[3,32,256]{2,1,0:T(8,128)}, f32[3,64,128]{2,1,0:T(8,128)}, f32[3,64,128]{2,1,0:T(8,128)}) custom-call(f32[19,32,256]{2,1,0:T(8,128)} %pop_ref.1, f32[3,8192]{1,0:T(4,128)} %pos_ref.1, f32[3,8192]{1,0:T(4,128)} %vel_ref.1, s32[64,128]{1,0:T(8,128)} %bitcast.1, s32[2,8192]{1,0:T(2,128)} %part_ref.1, ...), custom_call_target="tpu_custom_call" | custom-call | tf_op jit(solution)/shard_map/pallas_call | solution.py:654
  24.6 2.3 %shard_map.86 = (f32[19,32,256]{2,1,0:T(8,128)}, f32[3,8192]{1,0:T(4,128)}, f32[3,8192]{1,0:T(4,128)}) custom-call(f32[19,32,256]{2,1,0:T(8,128)} %get-tuple-element.7.passed_in, f32[3,32,256]{2,1,0:T(8,128)} %get-tuple-element.8.force_in, f32[3,64,128]{2,1,0:T(8,128)} %get-tuple-element.9.moved_in, f32[3,64,128]{2,1,0:T(8,128)} %get-tuple-element.10.vel_in), custom_call_target="tpu_custom_call" | custom-call | tf_op jit(solution)/shard_map/pallas_call | solution.py:701
